TPU v7x, 128 devices: a whole 4x4x4 slice. The times are simulated.
128 devices in a mesh: dp: 32 (over x, z, core), mp: 4 (over y).
Axes of the slice: x: 4, y: 4, z: 4, core: 2. Of those that a mesh axis runs over, the one named last changes fastest.
Arguments:
- tokens: bfloat16 [8192, 1024], P('dp', 'mp'), may hold values from -6 to 6
- grad_out: bfloat16 [8192, 1024], P('dp', 'mp'), may hold values from -6 to 6
- gates: bfloat16 [8192, 2], P('dp'), may hold values from 0.099609375 to 0.8984375
- expert_ids: int32 [8192, 2], P('dp'), may hold values from 0 to 63, all different within a row; in each aligned block of 256 rows (0 to 255, 256 to 511, ...) at most 16 rows name the same one
- w_gate: bfloat16 [64, 1024, 4096], P('dp', None, 'mp'), may hold values from -0.1875 to 0.1875
- w_up: bfloat16 [64, 1024, 4096], P('dp', None, 'mp'), may hold values from -0.1875 to 0.1875
- w_down: bfloat16 [64, 4096, 1024], P('dp', 'mp'), may hold values from -0.09375 to 0.09375
Outputs:
- grad_tokens: bfloat16 [8192, 1024], P('dp', 'mp')
- grad_gates: float32 [8192, 2], P('dp')
- grad_w_gate: bfloat16 [64, 1024, 4096], P('dp', None, 'mp')
- grad_w_up: bfloat16 [64, 1024, 4096], P('dp', None, 'mp')
- grad_w_down: bfloat16 [64, 4096, 1024], P('dp', 'mp')
Inputs may be any that keep to these rules, and one draw needn't show every extreme that they name: `expert_ids`: among the 256 tokens of one index of dp no expert is named more than 16 times, and in some such block some expert is named exactly 16 times; the two experts of a token differ.
All inputs are finite; a program needn't handle non-finite values.
Results may differ from a plain program's by a relative error of at most 0.0058.
Values may be sent and summed in bfloat16 or wider, within the bound.
A program may use at most 128 MiB of HBM per device.

v0:
```python
import jax
import jax.numpy as jnp
from jax import lax
from jax.sharding import PartitionSpec as P


def on_device(tokens, grad_out, gates, expert_ids, w_gate, w_up, w_down):
    count_tokens = tokens.shape[0]
    width_share = tokens.shape[1]
    groups = lax.axis_size("dp")
    local_experts = w_gate.shape[0]
    width_full = w_down.shape[2]
    all_experts = local_experts * groups
    capacity = max(2, 4 * count_tokens // all_experts)
    total_slots = all_experts * capacity
    onehot = (
        expert_ids[:, :, None] == jnp.arange(all_experts, dtype=jnp.int32)[None, None, :]
    ).astype(jnp.int32)
    onehot = onehot.reshape(count_tokens * 2, all_experts)
    before = jnp.cumsum(onehot, axis=0) - onehot
    position = jnp.sum(before * onehot, axis=1)
    slot_of = expert_ids.reshape(-1) * capacity + position
    placed = slot_of[None, :] == jnp.arange(total_slots, dtype=jnp.int32)[:, None]
    placed = placed.astype(jnp.bfloat16).reshape(total_slots, count_tokens, 2)
    route = jnp.sum(placed.astype(jnp.float32), axis=2).astype(jnp.bfloat16)
    slot_gate = jnp.einsum("stk,tk->s", placed, gates, preferred_element_type=jnp.float32).astype(
        jnp.bfloat16
    )
    slot_gate = slot_gate.reshape(groups, local_experts * capacity)
    full_x, full_dy = (
        lax.all_gather(tokens, "mp", axis=1, tiled=True),
        lax.all_gather(grad_out, "mp", axis=1, tiled=True),
    )
    send_x = jnp.dot(route, full_x, preferred_element_type=jnp.float32).astype(jnp.bfloat16)
    send_dy = jnp.dot(route, full_dy, preferred_element_type=jnp.float32).astype(jnp.bfloat16)
    send_x = send_x.reshape(groups, local_experts * capacity, width_full)
    send_dy = send_dy.reshape(groups, local_experts * capacity, width_full)
    recv_x, recv_dy, recv_gate = (
        lax.all_to_all(send_x, "dp", split_axis=0, concat_axis=0, tiled=True),
        lax.all_to_all(send_dy, "dp", split_axis=0, concat_axis=0, tiled=True),
        lax.all_to_all(slot_gate, "dp", split_axis=0, concat_axis=0, tiled=True),
    )
    recv_x = recv_x.reshape(groups, local_experts, capacity, width_full)
    recv_dy = recv_dy.reshape(groups, local_experts, capacity, width_full)
    recv_gate = recv_gate.reshape(groups, local_experts, capacity)
    grads_gate = []
    grads_up = []
    grads_down = []
    input_parts = []
    gate_parts = []
    for expert in range(local_experts):
        rows_x = recv_x[:, expert]
        rows_dy = recv_dy[:, expert]
        rows_gate = recv_gate[:, expert]
        gate_pre = jnp.einsum(
            "scd,df->scf", rows_x, w_gate[expert], preferred_element_type=jnp.float32
        )
        up_pre = jnp.einsum("scd,df->scf", rows_x, w_up[expert], preferred_element_type=jnp.float32)
        sigmoid_gate = jax.nn.sigmoid(gate_pre)
        activated = gate_pre * sigmoid_gate
        hidden = (activated * up_pre).astype(jnp.bfloat16)
        output_part = jnp.einsum(
            "scf,fd->scd", hidden, w_down[expert], preferred_element_type=jnp.float32
        )
        gate_parts.append(jnp.sum(rows_dy.astype(jnp.float32) * output_part, axis=2))
        scaled = (rows_gate.astype(jnp.float32)[:, :, None] * rows_dy.astype(jnp.float32)).astype(
            jnp.bfloat16
        )
        hidden_grad = jnp.einsum(
            "scd,fd->scf", scaled, w_down[expert], preferred_element_type=jnp.float32
        )
        dgate = (
            hidden_grad * up_pre * sigmoid_gate * (1.0 + gate_pre * (1.0 - sigmoid_gate))
        ).astype(jnp.bfloat16)
        dup = (hidden_grad * activated).astype(jnp.bfloat16)
        grads_down.append(
            jnp.einsum("scf,scd->fd", hidden, scaled, preferred_element_type=jnp.float32).astype(
                jnp.bfloat16
            )
        )
        grads_gate.append(
            jnp.einsum("scd,scf->df", rows_x, dgate, preferred_element_type=jnp.float32).astype(
                jnp.bfloat16
            )
        )
        grads_up.append(
            jnp.einsum("scd,scf->df", rows_x, dup, preferred_element_type=jnp.float32).astype(
                jnp.bfloat16
            )
        )
        input_parts.append(
            jnp.einsum("scf,df->scd", dgate, w_gate[expert], preferred_element_type=jnp.float32)
            + jnp.einsum("scf,df->scd", dup, w_up[expert], preferred_element_type=jnp.float32)
        )
    gate_stack = jnp.stack(gate_parts, axis=1)
    input_stack = jnp.stack(input_parts, axis=1)
    gate_total = lax.psum(gate_stack, "mp")
    back_gates = lax.all_to_all(gate_total, "dp", split_axis=0, concat_axis=0, tiled=True)
    back_gates = back_gates.reshape(total_slots)
    grad_gates = jnp.take(back_gates, slot_of, axis=0).reshape(count_tokens, 2)
    input_share = lax.psum_scatter(input_stack, "mp", scatter_dimension=3, tiled=True)
    back_rows = lax.all_to_all(input_share, "dp", split_axis=0, concat_axis=0, tiled=True)
    back_rows = back_rows.reshape(total_slots, width_share)
    picked = jnp.take(back_rows, slot_of, axis=0).reshape(count_tokens, 2, width_share)
    grad_tokens = jnp.sum(picked, axis=1).astype(jnp.bfloat16)
    return (
        grad_tokens,
        grad_gates,
        jnp.stack(grads_gate, axis=0),
        jnp.stack(grads_up, axis=0),
        jnp.stack(grads_down, axis=0),
    )


def solution(mesh):
    placed = (
        P("dp", "mp"),
        P("dp", "mp"),
        P("dp", None),
        P("dp", None),
        P("dp", None, "mp"),
        P("dp", None, "mp"),
        P("dp", "mp", None),
    )
    return jax.shard_map(
        on_device,
        mesh=mesh,
        in_specs=placed,
        out_specs=(
            P("dp", "mp"),
            P("dp", None),
            P("dp", None, "mp"),
            P("dp", None, "mp"),
            P("dp", "mp", None),
        ),
        check_vma=False,
    )
```

profile of v0, /device:TPU:1, one launch (start us, length us, event | category | flops | bytes accessed | tf_op | source)
XLA Modules:
  0.0 213.9 jit_solution(18338866497481159757)
XLA Ops:
  11.4 9.4 %all-to-all-start = ((bf16[32,1,32]{2,1,0:T(2,128)(2,1)}), bf16[32,1,32]{2,1,0:T(2,128)(2,1)S(1)}, u32[]{:S(2)}, u32[]{:S(2)}) async-start(bf16[32,1,32]{2,1,0:T(2,128)(2,1)} %all_to_all.24), calls=%async_computation | async-start | bytes 32768 | tf_op jit(solution)/shard_map/all_to_all | solution.py:41
  21.3 11.1 %all_gather.7 = bf16[256,1024]{1,0:T(8,128)(2,1)S(1)} all-gather(bf16[256,256]{1,0:T(8,128)(2,1)S(1)} %copy-done.9), channel_id=1, replica_groups=mesh['dp'=32,'mp'=4] {'mp'}, dimensions={1}, use_global_device_ids=true | all-gather | bytes 655360 | tf_op jit(solution)/shard_map/all_gather | solution.py:31
  34.5 9.7 %all-to-all-start.2 = ((bf16[32,32,1024]{2,1,0:T(8,128)(2,1)}), bf16[32,32,1024]{2,1,0:T(8,128)(2,1)S(1)}, u32[]{:S(2)}, u32[]{:S(2)}) async-start(bf16[32,32,1024]{2,1,0:T(8,128)(2,1)} %bitcast.10), calls=%async_computation.2 | async-start | bytes 4194304 | tf_op jit(solution)/shard_map/all_to_all | solution.py:39
  44.2 11.5 %all_gather.6 = bf16[256,1024]{1,0:T(8,128)(2,1)S(1)} all-gather(bf16[256,256]{1,0:T(8,128)(2,1)S(1)} %copy-done.10), channel_id=1, replica_groups=mesh['dp'=32,'mp'=4] {'mp'}, dimensions={1}, use_global_device_ids=true | all-gather | bytes 655360 | tf_op jit(solution)/shard_map/all_gather | solution.py:32
  57.8 14.8 %all-to-all-done.2 = bf16[32,32,1024]{2,1,0:T(8,128)(2,1)S(1)} async-done(((bf16[32,32,1024]{2,1,0:T(8,128)(2,1)}), bf16[32,32,1024]{2,1,0:T(8,128)(2,1)S(1)}, u32[]{:S(2)}, u32[]{:S(2)}) %all-to-all-start.2) | async-done | bytes 2097184 | tf_op jit(solution)/shard_map/all_to_all | solution.py:39
  72.5 5.2 %all-to-all-start.1 = ((bf16[32,32,1024]{2,1,0:T(8,128)(2,1)}), bf16[32,32,1024]{2,1,0:T(8,128)(2,1)}, u32[]{:S(2)}, u32[]{:S(2)}) async-start(bf16[32,32,1024]{2,1,0:T(8,128)(2,1)} %bitcast.5), calls=%async_computation.1 | async-start | bytes 4194304 | tf_op jit(solution)/shard_map/all_to_all | solution.py:40
  78.9 4.3 %fusion.12 = f32[32,16,1024]{2,1,0:T(8,128)} fusion(bf16[2,1024,1024]{2,1,0:T(8,128)(2,1)} %param.11, bf16[32,2,16,1024]{3,2,1,0:T(8,128)(2,1)S(1)} %bitcast.215), kind=kOutput, calls=%fused_computation.28 | convolution fusion | flops 1073741824 | bytes 5242880 | tf_op jit(solution)/shard_map/scd,df->scf/dot_general | solution.py:55
  83.3 2.6 %fusion.24 = f32[32,16,1024]{2,1,0:T(8,128)} fusion(bf16[2,1024,1024]{2,1,0:T(8,128)(2,1)S(1)} %copy-done.12, bf16[32,2,16,1024]{3,2,1,0:T(8,128)(2,1)S(1)} %bitcast.216), kind=kOutput, calls=%fused_computation.40 | convolution fusion | flops 1073741824 | bytes 5242880 | tf_op jit(solution)/shard_map/scd,df->scf/dot_general | solution.py:55
  85.8 20.3 %all-to-all-done.1 = bf16[32,32,1024]{2,1,0:T(8,128)(2,1)} async-done(((bf16[32,32,1024]{2,1,0:T(8,128)(2,1)}), bf16[32,32,1024]{2,1,0:T(8,128)(2,1)}, u32[]{:S(2)}, u32[]{:S(2)}) %all-to-all-start.1) | async-done | bytes 2097184 | tf_op jit(solution)/shard_map/all_to_all | solution.py:40
  106.2 3.4 %fusion.20 = f32[32,16,1024]{2,1,0:T(8,128)S(1)} fusion(bf16[2,1024,1024]{2,1,0:T(8,128)(2,1)} %param.13, f32[32,16]{1,0:T(8,128)S(1)} %copy.79, bf16[32,2,16,1024]{3,2,1,0:T(8,128)(2,1)} %bitcast.6), kind=kOutput, calls=%fused_computation.36 | convolution fusion | flops 1075314688 | bytes 5244928 | tf_op jit(solution)/shard_map/scd,fd->scf/dot_general | solution.py:69
  110.0 3.0 %multiply_convert_fusion = (bf16[32,16,1024]{2,1,0:T(8,128)(2,1)}, bf16[32,16,1024]{2,1,0:T(8,128)(2,1)S(1)}, bf16[32,16,1024]{2,1,0:T(8,128)(2,1)S(1)}) fusion(f32[32,16,1024]{2,1,0:T(8,128)S(1)} %copy-done.19, f32[32,16,1024]{2,1,0:T(8,128)S(1)} %fusion.20, bf16[2,1024,1024]{2,1,0:T(8,128)(2,1)S(1)} %copy-done.14, bf16[32,2,16,1024]{3,2,1,0:T(8,128)(2,1)S(1)} %bitcast.217), kind=kOutput, calls=%fused_computation.50 | convolution fusion | flops 1081606144 | bytes 10485760 | tf_op jit(solution)/shard_map/scd,df->scf/dot_general | solution.py:58
  116.2 2.7 %fusion.32 = f32[32,16,1024]{2,1,0:T(8,128)S(1)} fusion(bf16[2,1024,1024]{2,1,0:T(8,128)(2,1)S(1)} %copy-done.15, f32[32,16]{1,0:T(8,128)S(1)} %copy.76, bf16[32,2,16,1024]{3,2,1,0:T(8,128)(2,1)} %bitcast.6), kind=kOutput, calls=%fused_computation.48 | convolution fusion | flops 1075314688 | bytes 5259264 | tf_op jit(solution)/shard_map/scd,fd->scf/dot_general | solution.py:69
  118.9 3.0 %multiply_convert_fusion.1 = (bf16[32,16,1024]{2,1,0:T(8,128)(2,1)}, bf16[32,16,1024]{2,1,0:T(8,128)(2,1)S(1)}, bf16[32,16,1024]{2,1,0:T(8,128)(2,1)S(1)}) fusion(f32[32,16,1024]{2,1,0:T(8,128)S(1)} %copy-done.18, f32[32,16,1024]{2,1,0:T(8,128)S(1)} %fusion.32, bf16[2,1024,1024]{2,1,0:T(8,128)(2,1)S(1)} %copy-done.14, ...), kind=kOutput, calls=%fused_computation.51 | convolution fusion | flops 1081606144 | bytes 10485760 | tf_op jit(solution)/shard_map/scd,df->scf/dot_general | solution.py:58
  128.6 3.7 %fusion.7 = f32[32,16]{1,0:T(8,128)S(1)} fusion(bf16[32,16,1024]{2,1,0:T(8,128)(2,1)} %get-tuple-element.25, bf16[2,1024,1024]{2,1,0:T(8,128)(2,1)} %param.13, bf16[32,2,16,1024]{3,2,1,0:T(8,128)(2,1)} %bitcast.6), kind=kOutput, calls=%fused_computation.23 | convolution fusion | flops 1075314176 | bytes 4196352 | tf_op jit(solution)/shard_map/scf,fd->scd/dot_general | solution.py:62
  135.0 17.0 %psum.7 = f32[32,2,16]{2,1,0:T(2,128)} all-reduce(f32[32,2,16]{2,1,0:T(2,128)S(1)} %pad_maximum_fusion.4), channel_id=1, replica_groups=mesh['dp'=32,'mp'=4] {'mp'}, use_global_device_ids=true, to_apply=%region_8.9 | all-reduce | flops 1024 | bytes 8192 | tf_op jit(solution)/shard_map/psum | solution.py:97
  151.9 7.1 %all-to-all-start.4 = ((f32[32,2,16]{2,1,0:T(2,128)}), f32[32,2,16]{2,1,0:T(2,128)}, u32[]{:S(2)}, u32[]{:S(2)}) async-start(f32[32,2,16]{2,1,0:T(2,128)} %psum.7), calls=%async_computation.5 | async-start | bytes 65536 | tf_op jit(solution)/shard_map/all_to_all | solution.py:98
  159.0 4.0 %fusion.51 = bf16[1,1024,1024]{2,1,0:T(8,128)(2,1)} fusion(bf16[32,16,1024]{2,1,0:T(8,128)(2,1)} %copy-done.20, bf16[32,2,16,1024]{3,2,1,0:T(8,128)(2,1)S(1)} %bitcast.219), kind=kOutput, calls=%fused_computation.80 | convolution fusion | flops 1074790400 | bytes 4194304 | tf_op jit(solution)/shard_map/scd,scf->df/dot_general | solution.py:82
  163.0 2.6 %fusion.50 = bf16[1,1024,1024]{2,1,0:T(8,128)(2,1)} fusion(bf16[32,16,1024]{2,1,0:T(8,128)(2,1)S(1)} %copy-done.22, bf16[32,2,16,1024]{3,2,1,0:T(8,128)(2,1)S(1)} %bitcast.220), kind=kOutput, calls=%fused_computation.79 | convolution fusion | flops 1074790400 | bytes 4194304 | tf_op jit(solution)/shard_map/scd,scf->df/dot_general | solution.py:82
  165.7 4.0 %fusion.55 = bf16[1,1024,1024]{2,1,0:T(8,128)(2,1)} fusion(bf16[32,16,1024]{2,1,0:T(8,128)(2,1)S(1)} %copy-done.23, f32[32,16]{1,0:T(8,128)S(1)} %copy.79, bf16[32,2,16,1024]{3,2,1,0:T(8,128)(2,1)} %bitcast.6), kind=kOutput, calls=%fused_computation.84 | convolution fusion | flops 1076363264 | bytes 4196352 | tf_op jit(solution)/shard_map/scf,scd->fd/dot_general | solution.py:77
  169.7 3.9 %fusion.54 = bf16[1,1024,1024]{2,1,0:T(8,128)(2,1)} fusion(bf16[32,16,1024]{2,1,0:T(8,128)(2,1)S(1)} %copy-done.25, f32[32,16]{1,0:T(8,128)S(1)} %copy.76, bf16[32,2,16,1024]{3,2,1,0:T(8,128)(2,1)} %bitcast.6), kind=kOutput, calls=%fused_computation.83 | convolution fusion | flops 1076363264 | bytes 4196352 | tf_op jit(solution)/shard_map/scf,scd->fd/dot_general | solution.py:77
  173.6 2.6 %fusion.53 = bf16[1,1024,1024]{2,1,0:T(8,128)(2,1)} fusion(bf16[32,16,1024]{2,1,0:T(8,128)(2,1)S(1)} %get-tuple-element.27, bf16[32,2,16,1024]{3,2,1,0:T(8,128)(2,1)S(1)} %bitcast.221), kind=kOutput, calls=%fused_computation.82 | convolution fusion | flops 1074790400 | bytes 4194304 | tf_op jit(solution)/shard_map/scd,scf->df/dot_general | solution.py:87
  178.6 7.5 %all-to-all-start.3 = ((f32[32,2,16,256]{3,2,1,0:T(8,128)}), f32[32,2,16,256]{3,2,1,0:T(8,128)S(1)}, u32[]{:S(2)}, u32[]{:S(2)}) async-start(f32[32,2,16,256]{3,2,1,0:T(8,128)} %copy.82), calls=%async_computation.4 | async-start | bytes 2097152 | tf_op jit(solution)/shard_map/all_to_all | solution.py:102
  186.1 2.7 %fusion.52 = bf16[1,1024,1024]{2,1,0:T(8,128)(2,1)S(1)} fusion(bf16[32,16,1024]{2,1,0:T(8,128)(2,1)} %copy-done.17, bf16[32,2,16,1024]{3,2,1,0:T(8,128)(2,1)S(1)} %bitcast.222), kind=kOutput, calls=%fused_computation.81 | convolution fusion | flops 1074790400 | bytes 4194304 | tf_op jit(solution)/shard_map/scd,scf->df/dot_general | solution.py:87
  193.2 3.7 %pad_maximum_fusion.1 = (bf16[2,1024,1024]{2,1,0:T(8,128)(2,1)}, bf16[2,1024,1024]{2,1,0:T(8,128)(2,1)}) fusion(bf16[1,1024,1024]{2,1,0:T(8,128)(2,1)S(1)} %copy-done.4, bf16[1,1024,1024]{2,1,0:T(8,128)(2,1)S(1)} %copy-done.5, bf16[1,1024,1024]{2,1,0:T(8,128)(2,1)S(1)} %copy-done.6, bf16[1,1024,1024]{2,1,0:T(8,128)(2,1)S(1)} %fusion.52), kind=kLoop, calls=%fused_computation.3 | loop fusion | flops 4194304 | bytes 16777216 | tf_op jit(solution)/shard_map/stack | solution.py:109
  (100 shorter events, 39.7 us)
Async XLA Ops:
  7.2 3.1 %copy-start = (bf16[256,2]{0,1:T(2,128)(2,1)S(1)}, bf16[256,2]{0,1:T(2,128)(2,1)}, u32[]{:S(2)}) copy-start(bf16[256,2]{0,1:T(2,128)(2,1)} %param.9) | copy-start | bytes 3076
  7.2 14.1 %copy-start.9 = (bf16[256,256]{1,0:T(8,128)(2,1)S(1)}, bf16[256,256]{1,0:T(8,128)(2,1)}, u32[]{:S(2)}) copy-start(bf16[256,256]{1,0:T(8,128)(2,1)} %param.7) | copy-start | bytes 393220
  11.4 23.0 %all-to-all-start = ((bf16[32,1,32]{2,1,0:T(2,128)(2,1)}), bf16[32,1,32]{2,1,0:T(2,128)(2,1)S(1)}, u32[]{:S(2)}, u32[]{:S(2)}) async-start(bf16[32,1,32]{2,1,0:T(2,128)(2,1)} %all_to_all.24), calls=%async_computation | async-start | bytes 32768 | tf_op jit(solution)/shard_map/all_to_all | solution.py:41
  34.4 9.7 %copy-start.10 = (bf16[256,256]{1,0:T(8,128)(2,1)S(1)}, bf16[256,256]{1,0:T(8,128)(2,1)}, u32[]{:S(2)}) copy-start(bf16[256,256]{1,0:T(8,128)(2,1)} %param.8) | copy-start | bytes 393220
  34.5 38.1 %all-to-all-start.2 = ((bf16[32,32,1024]{2,1,0:T(8,128)(2,1)}), bf16[32,32,1024]{2,1,0:T(8,128)(2,1)S(1)}, u32[]{:S(2)}, u32[]{:S(2)}) async-start(bf16[32,32,1024]{2,1,0:T(8,128)(2,1)} %bitcast.10), calls=%async_computation.2 | async-start | bytes 4194304 | tf_op jit(solution)/shard_map/all_to_all | solution.py:39
  72.5 33.6 %all-to-all-start.1 = ((bf16[32,32,1024]{2,1,0:T(8,128)(2,1)}), bf16[32,32,1024]{2,1,0:T(8,128)(2,1)}, u32[]{:S(2)}, u32[]{:S(2)}) async-start(bf16[32,32,1024]{2,1,0:T(8,128)(2,1)} %bitcast.5), calls=%async_computation.1 | async-start | bytes 4194304 | tf_op jit(solution)/shard_map/all_to_all | solution.py:40
  77.7 98.5 %reduce-scatter.2.cloned.1.call-start = ((), (), s32[]{:S(2)}) async-start(), calls=%async_computation.6 | async-start | bytes 5242880 | tf_op jit(solution)/shard_map/reduce_scatter | solution.py:101
  78.9 4.3 %copy-start.12 = (bf16[2,1024,1024]{2,1,0:T(8,128)(2,1)S(1)}, bf16[2,1024,1024]{2,1,0:T(8,128)(2,1)}, u32[]{:S(2)}) copy-start(bf16[2,1024,1024]{2,1,0:T(8,128)(2,1)} %param.11) | copy-start | bytes 12582916
  106.2 3.4 %copy-start.14 = (bf16[2,1024,1024]{2,1,0:T(8,128)(2,1)S(1)}, bf16[2,1024,1024]{2,1,0:T(8,128)(2,1)}, u32[]{:S(2)}) copy-start(bf16[2,1024,1024]{2,1,0:T(8,128)(2,1)} %param.12) | copy-start | bytes 12582916
  106.2 3.8 %copy-start.19 = (f32[32,16,1024]{2,1,0:T(8,128)S(1)}, f32[32,16,1024]{2,1,0:T(8,128)}, u32[]{:S(2)}) copy-start(f32[32,16,1024]{2,1,0:T(8,128)} %fusion.12) | copy-start | bytes 6291460
  110.0 4.0 %copy-start.13 = (bf16[2,1024,1024]{2,1,0:T(8,128)(2,1)S(1)}, bf16[2,1024,1024]{2,1,0:T(8,128)(2,1)}, u32[]{:S(2)}) copy-start(bf16[2,1024,1024]{2,1,0:T(8,128)(2,1)} %param.11) | copy-start | bytes 12582916
  128.6 3.7 %copy-start.16 = (bf16[2,1024,1024]{2,1,0:T(8,128)(2,1)S(1)}, bf16[2,1024,1024]{2,1,0:T(8,128)(2,1)}, u32[]{:S(2)}) copy-start(bf16[2,1024,1024]{2,1,0:T(8,128)(2,1)} %param.13) | copy-start | bytes 12582916
  128.6 3.7 %copy-start.24 = (bf16[32,16,1024]{2,1,0:T(8,128)(2,1)S(1)}, bf16[32,16,1024]{2,1,0:T(8,128)(2,1)}, u32[]{:S(2)}) copy-start(bf16[32,16,1024]{2,1,0:T(8,128)(2,1)} %get-tuple-element.22) | copy-start | bytes 3145732
  151.9 26.7 %all-to-all-start.4 = ((f32[32,2,16]{2,1,0:T(2,128)}), f32[32,2,16]{2,1,0:T(2,128)}, u32[]{:S(2)}, u32[]{:S(2)}) async-start(f32[32,2,16]{2,1,0:T(2,128)} %psum.7), calls=%async_computation.5 | async-start | bytes 65536 | tf_op jit(solution)/shard_map/all_to_all | solution.py:98
  159.0 4.0 %copy-start.22 = (bf16[32,16,1024]{2,1,0:T(8,128)(2,1)S(1)}, bf16[32,16,1024]{2,1,0:T(8,128)(2,1)}, u32[]{:S(2)}) copy-start(bf16[32,16,1024]{2,1,0:T(8,128)(2,1)} %copy-done.21) | copy-start | bytes 3145732
  165.7 4.0 %copy-start.25 = (bf16[32,16,1024]{2,1,0:T(8,128)(2,1)S(1)}, bf16[32,16,1024]{2,1,0:T(8,128)(2,1)}, u32[]{:S(2)}) copy-start(bf16[32,16,1024]{2,1,0:T(8,128)(2,1)} %get-tuple-element.22) | copy-start | bytes 3145732
  178.6 24.4 %all-to-all-start.3 = ((f32[32,2,16,256]{3,2,1,0:T(8,128)}), f32[32,2,16,256]{3,2,1,0:T(8,128)S(1)}, u32[]{:S(2)}, u32[]{:S(2)}) async-start(f32[32,2,16,256]{3,2,1,0:T(8,128)} %copy.82), calls=%async_computation.4 | async-start | bytes 2097152 | tf_op jit(solution)/shard_map/all_to_all | solution.py:102
  186.1 2.7 %copy-start.2 = (bf16[1,1024,1024]{2,1,0:T(8,128)(2,1)S(1)}, bf16[1,1024,1024]{2,1,0:T(8,128)(2,1)}, u32[]{:S(2)}) copy-start(bf16[1,1024,1024]{2,1,0:T(8,128)(2,1)} %fusion.55) | copy-start | bytes 6291460
  186.1 2.7 %copy-start.3 = (bf16[1,1024,1024]{2,1,0:T(8,128)(2,1)S(1)}, bf16[1,1024,1024]{2,1,0:T(8,128)(2,1)}, u32[]{:S(2)}) copy-start(bf16[1,1024,1024]{2,1,0:T(8,128)(2,1)} %fusion.54) | copy-start | bytes 6291460
  188.8 3.7 %copy-start.5 = (bf16[1,1024,1024]{2,1,0:T(8,128)(2,1)S(1)}, bf16[1,1024,1024]{2,1,0:T(8,128)(2,1)}, u32[]{:S(2)}) copy-start(bf16[1,1024,1024]{2,1,0:T(8,128)(2,1)} %fusion.50) | copy-start | bytes 6291460
  188.9 4.4 %copy-start.6 = (bf16[1,1024,1024]{2,1,0:T(8,128)(2,1)S(1)}, bf16[1,1024,1024]{2,1,0:T(8,128)(2,1)}, u32[]{:S(2)}) copy-start(bf16[1,1024,1024]{2,1,0:T(8,128)(2,1)} %fusion.53) | copy-start | bytes 6291460
  193.2 4.6 %copy-start.11 = (s32[1024]{0:T(1024)S(1)}, s32[1024]{0:T(1024)}, u32[]{:S(2)}) copy-start(s32[1024]{0:T(1024)} %pad_clamp_fusion) | copy-start | bytes 12292
  196.9 3.3 %copy-start.8 = (s32[256,2]{1,0:T(8,128)S(1)}, s32[256,2]{1,0:T(8,128)}, u32[]{:S(2)}) copy-start(s32[256,2]{1,0:T(8,128)} %copy-done.7) | copy-start | bytes 6148
  203.0 4.0 %copy-start.1 = (bf16[256,2]{0,1:T(2,128)(2,1)S(1)}, bf16[256,2]{0,1:T(2,128)(2,1)}, u32[]{:S(2)}) copy-start(bf16[256,2]{0,1:T(2,128)(2,1)} %param.9) | copy-start | bytes 3076
  (8 other events, 16.2 us)
Sparse Core Ops, SparseCore 0:
  128.7 44.9 reduce-scatter.1
where the time goes:
time: 215 us; the launch traced here: 214 us
  matrix products  55 us (26%)
  blocking collectives  39.6 us (18%)
  starting transfers between devices  39.1 us (18%)
  waiting for transfers between devices  37.1 us (17%)
  local copies, waits for them, and re-layouts  15.2 us (7%)
  between operations  14.4 us (7%)
  other arithmetic  13.4 us (6%)
    all_to_all x1, waiting for transfers between devices, on_device(): lax.all_to_all(send_dy, 'dp', split_axis=0, concat_axis=0, tiled=True)  20.3 us
    psum x1, blocking collectives, on_device(): gate_total = lax.psum(gate_stack, 'mp')  17 us
    all_to_all x1, waiting for transfers between devices, on_device(): lax.all_to_all(send_x, 'dp', split_axis=0, concat_axis=0, tiled=True)  14.8 us
    all_gather x1, blocking collectives, on_device(): lax.all_gather(grad_out, 'mp', axis=1, tiled=True)  11.5 us
    all_gather x1, blocking collectives, on_device(): lax.all_gather(tokens, 'mp', axis=1, tiled=True)  11.1 us
    all_to_all x1, starting transfers between devices, on_device(): lax.all_to_all(send_x, 'dp', split_axis=0, concat_axis=0, tiled=True)  9.72 us
    all_to_all x1, starting transfers between devices, on_device(): lax.all_to_all(slot_gate, 'dp', split_axis=0, concat_axis=0, tiled=True)  9.42 us
    dot_general x2, matrix products, on_device(): jnp.einsum('scf,scd->fd', hidden, scaled, preferred_element_type=jnp.floa...  7.93 us
  transfers between devices with their start and end apart: 6, of which 3 were waited for; matrix products, arithmetic and copies ran while one was open for 24% of the time, Pallas kernels for 0%

commit v1 on v0

--- a/solution.py
+++ b/solution.py
@@ -94,7 +94,11 @@
         )
     gate_stack = jnp.stack(gate_parts, axis=1)
     input_stack = jnp.stack(input_parts, axis=1)
-    gate_total = lax.psum(gate_stack, "mp")
+    gate_total = gate_stack
+    for hop in (1, 2):
+        gate_total = gate_total + lax.ppermute(
+            gate_total, "mp", [(dev, dev ^ hop) for dev in range(4)]
+        )
     back_gates = lax.all_to_all(gate_total, "dp", split_axis=0, concat_axis=0, tiled=True)
     back_gates = back_gates.reshape(total_slots)
     grad_gates = jnp.take(back_gates, slot_of, axis=0).reshape(count_tokens, 2)

time: 215 us -> 212 us (0.986)
  blocking collectives: 39.6 us -> 22.6 us
  waiting for transfers between devices: 37.1 us -> 50.2 us
  starting transfers between devices: 39.1 us -> 42.3 us
    psum x1 -> x0, blocking collectives: 17 us -> none  [on_device(): gate_total = lax.psum(gate_stack, 'mp')]
    reduce_scatter x1, waiting for transfers between devices: 0.01 us -> 12.2 us  [on_device(): lax.psum_scatter(input_stack, 'mp', scatter_dimension=3, tiled=True)]
    ppermute x0 -> x2, starting transfers between devices: none -> 4.24 us  [on_device(): lax.ppermute(gate_total, 'mp', [(dev, dev ^ hop) for dev in range(4)])]
  transfers between devices with their start and end apart: 6 -> 8, of which waited for: 3 -> 4; matrix products, arithmetic and copies ran while one was open for 24% -> 24% of each run, Pallas kernels for 0% -> 0%
where the time goes in v1:
time: 212 us; the launch traced here: 211 us
  matrix products  53.6 us (25%)
  waiting for transfers between devices  50.2 us (24%)
  starting transfers between devices  42.3 us (20%)
  blocking collectives  22.6 us (11%)
  between operations  14.4 us (7%)
  other arithmetic  14.1 us (7%)
  local copies, waits for them, and re-layouts  13.8 us (7%)
    all_to_all x1, waiting for transfers between devices, on_device(): lax.all_to_all(send_dy, 'dp', split_axis=0, concat_axis=0, tiled=True)  20.3 us
    all_to_all x1, waiting for transfers between devices, on_device(): lax.all_to_all(send_x, 'dp', split_axis=0, concat_axis=0, tiled=True)  14.8 us
    reduce_scatter x1, waiting for transfers between devices, on_device(): lax.psum_scatter(input_stack, 'mp', scatter_dimension=3, tiled=True)  12.2 us
    all_gather x1, blocking collectives, on_device(): lax.all_gather(grad_out, 'mp', axis=1, tiled=True)  11.5 us
    all_gather x1, blocking collectives, on_device(): lax.all_gather(tokens, 'mp', axis=1, tiled=True)  11.1 us
    all_to_all x1, starting transfers between devices, on_device(): lax.all_to_all(send_x, 'dp', split_axis=0, concat_axis=0, tiled=True)  9.72 us
    all_to_all x1, starting transfers between devices, on_device(): lax.all_to_all(slot_gate, 'dp', split_axis=0, concat_axis=0, tiled=True)  9.42 us
    dot_general x2, matrix products, on_device(): jnp.einsum('scf,scd->fd', hidden, scaled, preferred_element_type=jnp.floa...  7.82 us
  transfers between devices with their start and end apart: 8, of which 4 were waited for; matrix products, arithmetic and copies ran while one was open for 24% of the time, Pallas kernels for 0%

profile of v1, /device:TPU:1, one launch (start us, length us, event | category | flops | bytes accessed | tf_op | source)
XLA Modules:
  0.0 211.1 jit_solution(3256262611984160011)
XLA Ops:
  11.4 9.4 %all-to-all-start = ((bf16[32,1,32]{2,1,0:T(2,128)(2,1)}), bf16[32,1,32]{2,1,0:T(2,128)(2,1)S(1)}, u32[]{:S(2)}, u32[]{:S(2)}) async-start(bf16[32,1,32]{2,1,0:T(2,128)(2,1)} %all_to_all.24), calls=%async_computation | async-start | bytes 32768 | tf_op jit(solution)/shard_map/all_to_all | solution.py:41
  21.3 11.1 %all_gather.7 = bf16[256,1024]{1,0:T(8,128)(2,1)S(1)} all-gather(bf16[256,256]{1,0:T(8,128)(2,1)S(1)} %copy-done.9), channel_id=1, replica_groups=mesh['dp'=32,'mp'=4] {'mp'}, dimensions={1}, use_global_device_ids=true | all-gather | bytes 655360 | tf_op jit(solution)/shard_map/all_gather | solution.py:31
  34.5 9.7 %all-to-all-start.2 = ((bf16[32,32,1024]{2,1,0:T(8,128)(2,1)}), bf16[32,32,1024]{2,1,0:T(8,128)(2,1)S(1)}, u32[]{:S(2)}, u32[]{:S(2)}) async-start(bf16[32,32,1024]{2,1,0:T(8,128)(2,1)} %bitcast.10), calls=%async_computation.2 | async-start | bytes 4194304 | tf_op jit(solution)/shard_map/all_to_all | solution.py:39
  44.2 11.5 %all_gather.6 = bf16[256,1024]{1,0:T(8,128)(2,1)S(1)} all-gather(bf16[256,256]{1,0:T(8,128)(2,1)S(1)} %copy-done.10), channel_id=1, replica_groups=mesh['dp'=32,'mp'=4] {'mp'}, dimensions={1}, use_global_device_ids=true | all-gather | bytes 655360 | tf_op jit(solution)/shard_map/all_gather | solution.py:32
  57.8 14.8 %all-to-all-done.2 = bf16[32,32,1024]{2,1,0:T(8,128)(2,1)S(1)} async-done(((bf16[32,32,1024]{2,1,0:T(8,128)(2,1)}), bf16[32,32,1024]{2,1,0:T(8,128)(2,1)S(1)}, u32[]{:S(2)}, u32[]{:S(2)}) %all-to-all-start.2) | async-done | bytes 2097184 | tf_op jit(solution)/shard_map/all_to_all | solution.py:39
  72.5 5.2 %all-to-all-start.1 = ((bf16[32,32,1024]{2,1,0:T(8,128)(2,1)}), bf16[32,32,1024]{2,1,0:T(8,128)(2,1)}, u32[]{:S(2)}, u32[]{:S(2)}) async-start(bf16[32,32,1024]{2,1,0:T(8,128)(2,1)} %bitcast.5), calls=%async_computation.1 | async-start | bytes 4194304 | tf_op jit(solution)/shard_map/all_to_all | solution.py:40
  78.9 4.3 %fusion.12 = f32[32,16,1024]{2,1,0:T(8,128)} fusion(bf16[2,1024,1024]{2,1,0:T(8,128)(2,1)} %param.11, bf16[32,2,16,1024]{3,2,1,0:T(8,128)(2,1)S(1)} %bitcast.215), kind=kOutput, calls=%fused_computation.28 | convolution fusion | flops 1073741824 | bytes 5242880 | tf_op jit(solution)/shard_map/scd,df->scf/dot_general | solution.py:55
  85.9 20.3 %all-to-all-done.1 = bf16[32,32,1024]{2,1,0:T(8,128)(2,1)} async-done(((bf16[32,32,1024]{2,1,0:T(8,128)(2,1)}), bf16[32,32,1024]{2,1,0:T(8,128)(2,1)}, u32[]{:S(2)}, u32[]{:S(2)}) %all-to-all-start.1) | async-done | bytes 2097184 | tf_op jit(solution)/shard_map/all_to_all | solution.py:40
  106.2 3.4 %fusion.20 = f32[32,16,1024]{2,1,0:T(8,128)S(1)} fusion(bf16[2,1024,1024]{2,1,0:T(8,128)(2,1)} %param.13, f32[32,16]{1,0:T(8,128)S(1)} %copy.79, bf16[32,2,16,1024]{3,2,1,0:T(8,128)(2,1)} %bitcast.6), kind=kOutput, calls=%fused_computation.36 | convolution fusion | flops 1075314688 | bytes 5244928 | tf_op jit(solution)/shard_map/scd,fd->scf/dot_general | solution.py:69
  110.0 3.0 %multiply_convert_fusion = (bf16[32,16,1024]{2,1,0:T(8,128)(2,1)}, bf16[32,16,1024]{2,1,0:T(8,128)(2,1)S(1)}, bf16[32,16,1024]{2,1,0:T(8,128)(2,1)S(1)}) fusion(f32[32,16,1024]{2,1,0:T(8,128)S(1)} %copy-done.21, f32[32,16,1024]{2,1,0:T(8,128)S(1)} %fusion.20, bf16[2,1024,1024]{2,1,0:T(8,128)(2,1)S(1)} %copy-done.14, bf16[32,2,16,1024]{3,2,1,0:T(8,128)(2,1)S(1)} %bitcast.217), kind=kOutput, calls=%fused_computation.50 | convolution fusion | flops 1081606144 | bytes 10485760 | tf_op jit(solution)/shard_map/scd,df->scf/dot_general | solution.py:58
  115.6 2.7 %fusion.32 = f32[32,16,1024]{2,1,0:T(8,128)S(1)} fusion(bf16[2,1024,1024]{2,1,0:T(8,128)(2,1)S(1)} %copy-done.15, f32[32,16]{1,0:T(8,128)S(1)} %copy.76, bf16[32,2,16,1024]{3,2,1,0:T(8,128)(2,1)} %bitcast.6), kind=kOutput, calls=%fused_computation.48 | convolution fusion | flops 1075314688 | bytes 5259264 | tf_op jit(solution)/shard_map/scd,fd->scf/dot_general | solution.py:69
  118.3 3.0 %multiply_convert_fusion.1 = (bf16[32,16,1024]{2,1,0:T(8,128)(2,1)}, bf16[32,16,1024]{2,1,0:T(8,128)(2,1)S(1)}, bf16[32,16,1024]{2,1,0:T(8,128)(2,1)S(1)}) fusion(f32[32,16,1024]{2,1,0:T(8,128)S(1)} %copy-done.20, f32[32,16,1024]{2,1,0:T(8,128)S(1)} %fusion.32, bf16[2,1024,1024]{2,1,0:T(8,128)(2,1)S(1)} %copy-done.14, ...), kind=kOutput, calls=%fused_computation.51 | convolution fusion | flops 1081606144 | bytes 10485760 | tf_op jit(solution)/shard_map/scd,df->scf/dot_general | solution.py:58
  128.0 3.7 %fusion.7 = f32[32,16]{1,0:T(8,128)S(1)} fusion(bf16[32,16,1024]{2,1,0:T(8,128)(2,1)} %get-tuple-element.25, bf16[2,1024,1024]{2,1,0:T(8,128)(2,1)} %param.13, bf16[32,2,16,1024]{3,2,1,0:T(8,128)(2,1)} %bitcast.6), kind=kOutput, calls=%fused_computation.23 | convolution fusion | flops 1075314176 | bytes 4196352 | tf_op jit(solution)/shard_map/scf,fd->scd/dot_general | solution.py:62
  131.7 2.7 %fusion.4 = f32[32,16]{1,0:T(8,128)S(1)} fusion(bf16[32,16,1024]{2,1,0:T(8,128)(2,1)S(1)} %copy-done.25, bf16[2,1024,1024]{2,1,0:T(8,128)(2,1)S(1)} %copy-done.16, bf16[32,2,16,1024]{3,2,1,0:T(8,128)(2,1)} %bitcast.6), kind=kOutput, calls=%fused_computation.20 | convolution fusion | flops 1075314176 | bytes 4196352 | tf_op jit(solution)/shard_map/scf,fd->scd/dot_general | solution.py:62
  136.2 3.9 %fusion.55 = bf16[1,1024,1024]{2,1,0:T(8,128)(2,1)} fusion(bf16[32,16,1024]{2,1,0:T(8,128)(2,1)S(1)} %copy-done.24, f32[32,16]{1,0:T(8,128)S(1)} %copy.79, bf16[32,2,16,1024]{3,2,1,0:T(8,128)(2,1)} %bitcast.6), kind=kOutput, calls=%fused_computation.84 | convolution fusion | flops 1076363264 | bytes 4196352 | tf_op jit(solution)/shard_map/scf,scd->fd/dot_general | solution.py:77
  140.1 3.9 %fusion.54 = bf16[1,1024,1024]{2,1,0:T(8,128)(2,1)} fusion(bf16[32,16,1024]{2,1,0:T(8,128)(2,1)S(1)} %copy-done.25, f32[32,16]{1,0:T(8,128)S(1)} %copy.76, bf16[32,2,16,1024]{3,2,1,0:T(8,128)(2,1)} %bitcast.6), kind=kOutput, calls=%fused_computation.83 | convolution fusion | flops 1076363264 | bytes 4196352 | tf_op jit(solution)/shard_map/scf,scd->fd/dot_general | solution.py:77
  149.2 2.6 %fusion.50 = bf16[1,1024,1024]{2,1,0:T(8,128)(2,1)} fusion(bf16[32,16,1024]{2,1,0:T(8,128)(2,1)S(1)} %copy-done.23, bf16[32,2,16,1024]{3,2,1,0:T(8,128)(2,1)S(1)} %bitcast.220), kind=kOutput, calls=%fused_computation.79 | convolution fusion | flops 1074790400 | bytes 4194304 | tf_op jit(solution)/shard_map/scd,scf->df/dot_general | solution.py:82
  152.5 5.8 %all-to-all-start.4 = ((f32[32,2,16]{2,1,0:T(2,128)}), f32[32,2,16]{2,1,0:T(2,128)S(1)}, u32[]{:S(2)}, u32[]{:S(2)}) async-start(f32[32,2,16]{2,1,0:T(2,128)} %fusion.101), calls=%async_computation.5 | async-start | bytes 65536 | tf_op jit(solution)/shard_map/all_to_all | solution.py:102
  158.3 2.7 %fusion.53 = bf16[1,1024,1024]{2,1,0:T(8,128)(2,1)} fusion(bf16[32,16,1024]{2,1,0:T(8,128)(2,1)S(1)} %copy-done.19, bf16[32,2,16,1024]{3,2,1,0:T(8,128)(2,1)S(1)} %bitcast.221), kind=kOutput, calls=%fused_computation.82 | convolution fusion | flops 1074790400 | bytes 4194304 | tf_op jit(solution)/shard_map/scd,scf->df/dot_general | solution.py:87
  161.0 12.2 %reduce-scatter.2.cloned.1.call-done = f32[32,2,16,256]{3,2,0,1:T(8,128)} async-done(((f32[32,2,16,1024]{3,2,0,1:T(8,128)}), f32[32,2,16,256]{3,2,0,1:T(8,128)}) %reduce-scatter.2.cloned.1.call-update) | async-done | bytes 1048592 | tf_op jit(solution)/shard_map/reduce_scatter | solution.py:105
  175.6 7.8 %all-to-all-start.3 = ((f32[32,2,16,256]{3,2,1,0:T(8,128)}), f32[32,2,16,256]{3,2,1,0:T(8,128)S(1)}, u32[]{:S(2)}, u32[]{:S(2)}) async-start(f32[32,2,16,256]{3,2,1,0:T(8,128)} %copy.82), calls=%async_computation.4 | async-start | bytes 2097152 | tf_op jit(solution)/shard_map/all_to_all | solution.py:106
  183.4 2.7 %fusion.52 = bf16[1,1024,1024]{2,1,0:T(8,128)(2,1)S(1)} fusion(bf16[32,16,1024]{2,1,0:T(8,128)(2,1)} %copy-done.17, bf16[32,2,16,1024]{3,2,1,0:T(8,128)(2,1)S(1)} %bitcast.222), kind=kOutput, calls=%fused_computation.81 | convolution fusion | flops 1074790400 | bytes 4194304 | tf_op jit(solution)/shard_map/scd,scf->df/dot_general | solution.py:87
  190.4 3.7 %pad_maximum_fusion.1 = (bf16[2,1024,1024]{2,1,0:T(8,128)(2,1)}, bf16[2,1024,1024]{2,1,0:T(8,128)(2,1)}) fusion(bf16[1,1024,1024]{2,1,0:T(8,128)(2,1)S(1)} %copy-done.4, bf16[1,1024,1024]{2,1,0:T(8,128)(2,1)S(1)} %copy-done.5, bf16[1,1024,1024]{2,1,0:T(8,128)(2,1)S(1)} %copy-done.6, bf16[1,1024,1024]{2,1,0:T(8,128)(2,1)S(1)} %fusion.52), kind=kLoop, calls=%fused_computation.3 | loop fusion | flops 4194304 | bytes 16777216 | tf_op jit(solution)/shard_map/stack | solution.py:113
  197.4 2.8 %all-to-all-done.3 = f32[32,2,16,256]{3,2,1,0:T(8,128)S(1)} async-done(((f32[32,2,16,256]{3,2,1,0:T(8,128)}), f32[32,2,16,256]{3,2,1,0:T(8,128)S(1)}, u32[]{:S(2)}, u32[]{:S(2)}) %all-to-all-start.3) | async-done | bytes 1048608 | tf_op jit(solution)/shard_map/all_to_all | solution.py:106
  (105 shorter events, 43.9 us)
Async XLA Ops:
  7.2 3.1 %copy-start = (bf16[256,2]{0,1:T(2,128)(2,1)S(1)}, bf16[256,2]{0,1:T(2,128)(2,1)}, u32[]{:S(2)}) copy-start(bf16[256,2]{0,1:T(2,128)(2,1)} %param.9) | copy-start | bytes 3076
  7.2 14.1 %copy-start.9 = (bf16[256,256]{1,0:T(8,128)(2,1)S(1)}, bf16[256,256]{1,0:T(8,128)(2,1)}, u32[]{:S(2)}) copy-start(bf16[256,256]{1,0:T(8,128)(2,1)} %param.7) | copy-start | bytes 393220
  11.4 23.0 %all-to-all-start = ((bf16[32,1,32]{2,1,0:T(2,128)(2,1)}), bf16[32,1,32]{2,1,0:T(2,128)(2,1)S(1)}, u32[]{:S(2)}, u32[]{:S(2)}) async-start(bf16[32,1,32]{2,1,0:T(2,128)(2,1)} %all_to_all.24), calls=%async_computation | async-start | bytes 32768 | tf_op jit(solution)/shard_map/all_to_all | solution.py:41
  34.4 9.7 %copy-start.10 = (bf16[256,256]{1,0:T(8,128)(2,1)S(1)}, bf16[256,256]{1,0:T(8,128)(2,1)}, u32[]{:S(2)}) copy-start(bf16[256,256]{1,0:T(8,128)(2,1)} %param.8) | copy-start | bytes 393220
  34.5 38.1 %all-to-all-start.2 = ((bf16[32,32,1024]{2,1,0:T(8,128)(2,1)}), bf16[32,32,1024]{2,1,0:T(8,128)(2,1)S(1)}, u32[]{:S(2)}, u32[]{:S(2)}) async-start(bf16[32,32,1024]{2,1,0:T(8,128)(2,1)} %bitcast.10), calls=%async_computation.2 | async-start | bytes 4194304 | tf_op jit(solution)/shard_map/all_to_all | solution.py:39
  72.5 33.7 %all-to-all-start.1 = ((bf16[32,32,1024]{2,1,0:T(8,128)(2,1)}), bf16[32,32,1024]{2,1,0:T(8,128)(2,1)}, u32[]{:S(2)}, u32[]{:S(2)}) async-start(bf16[32,32,1024]{2,1,0:T(8,128)(2,1)} %bitcast.5), calls=%async_computation.1 | async-start | bytes 4194304 | tf_op jit(solution)/shard_map/all_to_all | solution.py:40
  77.7 95.5 %reduce-scatter.2.cloned.1.call-start = ((), (), s32[]{:S(2)}) async-start(), calls=%async_computation.6 | async-start | bytes 5242880 | tf_op jit(solution)/shard_map/reduce_scatter | solution.py:105
  78.9 4.4 %copy-start.12 = (bf16[2,1024,1024]{2,1,0:T(8,128)(2,1)S(1)}, bf16[2,1024,1024]{2,1,0:T(8,128)(2,1)}, u32[]{:S(2)}) copy-start(bf16[2,1024,1024]{2,1,0:T(8,128)(2,1)} %param.11) | copy-start | bytes 12582916
  106.2 3.4 %copy-start.14 = (bf16[2,1024,1024]{2,1,0:T(8,128)(2,1)S(1)}, bf16[2,1024,1024]{2,1,0:T(8,128)(2,1)}, u32[]{:S(2)}) copy-start(bf16[2,1024,1024]{2,1,0:T(8,128)(2,1)} %param.12) | copy-start | bytes 12582916
  106.2 3.8 %copy-start.21 = (f32[32,16,1024]{2,1,0:T(8,128)S(1)}, f32[32,16,1024]{2,1,0:T(8,128)}, u32[]{:S(2)}) copy-start(f32[32,16,1024]{2,1,0:T(8,128)} %fusion.12) | copy-start | bytes 6291460
  113.0 9.6 %copy-start.18 = (bf16[32,16,1024]{2,1,0:T(8,128)(2,1)}, bf16[32,16,1024]{2,1,0:T(8,128)(2,1)S(1)}, u32[]{:S(2)}) copy-start(bf16[32,16,1024]{2,1,0:T(8,128)(2,1)S(1)} %get-tuple-element.27) | copy-start | bytes 3145732
  128.0 3.7 %copy-start.16 = (bf16[2,1024,1024]{2,1,0:T(8,128)(2,1)S(1)}, bf16[2,1024,1024]{2,1,0:T(8,128)(2,1)}, u32[]{:S(2)}) copy-start(bf16[2,1024,1024]{2,1,0:T(8,128)(2,1)} %param.13) | copy-start | bytes 12582916
  128.0 3.7 %copy-start.25 = (bf16[32,16,1024]{2,1,0:T(8,128)(2,1)S(1)}, bf16[32,16,1024]{2,1,0:T(8,128)(2,1)}, u32[]{:S(2)}) copy-start(bf16[32,16,1024]{2,1,0:T(8,128)(2,1)} %get-tuple-element.22) | copy-start | bytes 3145732
  131.7 4.5 %copy-start.24 = (bf16[32,16,1024]{2,1,0:T(8,128)(2,1)S(1)}, bf16[32,16,1024]{2,1,0:T(8,128)(2,1)}, u32[]{:S(2)}) copy-start(bf16[32,16,1024]{2,1,0:T(8,128)(2,1)} %get-tuple-element.25) | copy-start | bytes 3145732
  134.5 12.2 %collective-permute-start = (f32[32,2,16]{2,1,0:T(2,128)S(1)}, f32[32,2,16]{2,1,0:T(2,128)S(1)}, u32[]{:S(2)}, u32[]{:S(2)}) collective-permute-start(f32[32,2,16]{2,1,0:T(2,128)S(1)} %pad_maximum_fusion.4), channel_id=1, source_target_pairs={{0,1},{1,0},{2,3},{3,2},{4,5},{5,4},{6,7},{7,6},{8,9},{9,8},{10,11... | collective-permute-start | bytes 12296 | tf_op jit(solution)/shard_map/ppermute | solution.py:99
  144.0 5.2 %copy-start.23 = (bf16[32,16,1024]{2,1,0:T(8,128)(2,1)S(1)}, bf16[32,16,1024]{2,1,0:T(8,128)(2,1)}, u32[]{:S(2)}) copy-start(bf16[32,16,1024]{2,1,0:T(8,128)(2,1)} %copy-done.22) | copy-start | bytes 3145732
  146.7 11.6 %copy-start.19 = (bf16[32,16,1024]{2,1,0:T(8,128)(2,1)S(1)}, bf16[32,16,1024]{2,1,0:T(8,128)(2,1)}, u32[]{:S(2)}) copy-start(bf16[32,16,1024]{2,1,0:T(8,128)(2,1)} %copy-done.18) | copy-start | bytes 3145732
  146.7 5.2 %collective-permute-start.1 = (f32[32,2,16]{2,1,0:T(2,128)S(1)}, f32[32,2,16]{2,1,0:T(2,128)S(1)}, u32[]{:S(2)}, u32[]{:S(2)}) collective-permute-start(f32[32,2,16]{2,1,0:T(2,128)S(1)} %fusion.84), channel_id=1, source_target_pairs={{0,2},{1,3},{2,0},{3,1},{4,6},{5,7},{6,4},{7,5},{8,10},{9,11},{10,... | collective-permute-start | bytes 12296 | tf_op jit(solution)/shard_map/ppermute | solution.py:99
  152.5 23.0 %all-to-all-start.4 = ((f32[32,2,16]{2,1,0:T(2,128)}), f32[32,2,16]{2,1,0:T(2,128)S(1)}, u32[]{:S(2)}, u32[]{:S(2)}) async-start(f32[32,2,16]{2,1,0:T(2,128)} %fusion.101), calls=%async_computation.5 | async-start | bytes 65536 | tf_op jit(solution)/shard_map/all_to_all | solution.py:102
  175.6 24.7 %all-to-all-start.3 = ((f32[32,2,16,256]{3,2,1,0:T(8,128)}), f32[32,2,16,256]{3,2,1,0:T(8,128)S(1)}, u32[]{:S(2)}, u32[]{:S(2)}) async-start(f32[32,2,16,256]{3,2,1,0:T(8,128)} %copy.82), calls=%async_computation.4 | async-start | bytes 2097152 | tf_op jit(solution)/shard_map/all_to_all | solution.py:106
  186.1 3.7 %copy-start.5 = (bf16[1,1024,1024]{2,1,0:T(8,128)(2,1)S(1)}, bf16[1,1024,1024]{2,1,0:T(8,128)(2,1)}, u32[]{:S(2)}) copy-start(bf16[1,1024,1024]{2,1,0:T(8,128)(2,1)} %fusion.50) | copy-start | bytes 6291460
  186.1 4.4 %copy-start.6 = (bf16[1,1024,1024]{2,1,0:T(8,128)(2,1)S(1)}, bf16[1,1024,1024]{2,1,0:T(8,128)(2,1)}, u32[]{:S(2)}) copy-start(bf16[1,1024,1024]{2,1,0:T(8,128)(2,1)} %fusion.53) | copy-start | bytes 6291460
  190.4 3.8 %copy-start.11 = (s32[1024]{0:T(1024)S(1)}, s32[1024]{0:T(1024)}, u32[]{:S(2)}) copy-start(s32[1024]{0:T(1024)} %pad_clamp_fusion) | copy-start | bytes 12292
  200.2 4.0 %copy-start.1 = (bf16[256,2]{0,1:T(2,128)(2,1)S(1)}, bf16[256,2]{0,1:T(2,128)(2,1)}, u32[]{:S(2)}) copy-start(bf16[256,2]{0,1:T(2,128)(2,1)} %param.9) | copy-start | bytes 3076
  (10 other events, 23.9 us)
Sparse Core Ops, SparseCore 0:
  128.1 45.0 reduce-scatter.1
